TPU v7x, 32 devices: a whole 2x2x4 slice. The times are simulated.
32 devices in a mesh: heads: 4 (over y, x), seq: 8 (over z, core).
Axes of the slice: x: 2, y: 2, z: 4, core: 2. Of those that a mesh axis runs over, the one named last changes fastest.
Arguments:
- tokens: bfloat16 [7168, 2048], P('seq'), may hold values from -6 to 6
- w_qkv: bfloat16 [2048, 3, 2048], P(None, None, 'heads'), may hold values from -0.1875 to 0.1875
- w_out: bfloat16 [2048, 2048], P('heads'), may hold values from -0.75 to 0.75
- w_up: bfloat16 [2048, 8192], P('seq', 'heads'), may hold values from -0.125 to 0.125
- w_down: bfloat16 [8192, 2048], P('heads', 'seq'), may hold values from -0.0625 to 0.0625
- gain_attn: float32 [2048], replicated, may hold values from 0.1 to 1.9
- gain_ffn: float32 [2048], replicated, may hold values from 0.1 to 1.9
- w_router: float32 [2048, 8], replicated, may hold values from -0.25 to 0.25
- head_quarters: int32 [5], replicated, may hold values from 1 to 4, as said below
- ffn_quarters: int32 [5], replicated, may hold values from 1 to 4, as said below
- router_targets: int32 [5, 2], replicated, may hold values from 0 to 3
- cotangent: bfloat16 [7168, 2048], P('seq'), may hold values from -6 to 6
Outputs:
- output: bfloat16 [7168, 2048], P('seq')
- grad_tokens: float32 [7168, 2048], P('seq')
- grad_qkv: float32 [2048, 3, 2048], P(None, None, 'heads')
- grad_out: float32 [2048, 2048], P('heads')
- grad_up: float32 [2048, 8192], P('seq', 'heads')
- grad_down: float32 [8192, 2048], P('heads', 'seq')
- grad_gain_attn: float32 [2048], replicated
- grad_gain_ffn: float32 [2048], replicated
- grad_router: float32 [2048, 8], replicated
Inputs may be any that keep to these rules, and one draw needn't show every extreme that they name: Sequence s uses the first head_quarters[s] * 4 heads; some sequence uses all heads and some a quarter of them. Sequence s uses the first ffn_quarters[s] * 2048 hidden units; some sequence uses all and some a quarter.
All inputs are finite; a program needn't handle non-finite values.
Results may differ from a plain program's by a relative error of at most 0.023.
Values may be sent and summed in bfloat16 or wider, within the bound.
No kernel may reach another device: no remote copies, remote signals or barrier semaphores. Data moves between devices by JAX's collectives and lax.ppermute only.
A program may use at most 256 MiB of HBM per device.

v0:
```python
import jax
import jax.numpy as jnp
from jax import lax
from jax.sharding import PartitionSpec as P

D = 2048
H = 16
HD = 128
FF = 8192
SHORT_DEV = 128
NSHORT = 3
NLONG = 2
LEVELS = 4
SEQS = 5
epsilon = 1e-05
highest = lax.Precision.HIGHEST


def normalize_parts(values):
    centered = values - jnp.mean(values, axis=-1, keepdims=True)
    inverse = lax.rsqrt(jnp.mean(centered * centered, axis=-1, keepdims=True) + epsilon)
    return (centered * inverse, inverse)


def normalize_back(grad_normed, normed_hat, inverse, gain):
    grad_hat = grad_normed * gain
    middle = (
        grad_hat
        - jnp.mean(grad_hat, axis=-1, keepdims=True)
        - normed_hat * jnp.mean(grad_hat * normed_hat, axis=-1, keepdims=True)
    )
    return (inverse * middle, jnp.sum(grad_normed * normed_hat, axis=0))


def rotate(values, cosine, sine, inverse_turn):
    row_count = values.shape[0]
    shaped = values.reshape(row_count, -1, HD)
    half_dim = HD // 2
    former = shaped[..., :half_dim]
    latter = shaped[..., half_dim:]
    if inverse_turn:
        turned = [former * cosine + latter * sine, latter * cosine - former * sine]
    else:
        turned = [former * cosine - latter * sine, latter * cosine + former * sine]
    return jnp.concatenate(turned, axis=-1).reshape(row_count, -1)


def gather_rows(keys, values):
    return (
        lax.all_gather(keys, "seq", axis=1, tiled=True),
        lax.all_gather(values, "seq", axis=1, tiled=True),
    )


def masked_scores(query, keys, first_pos):
    seq_number, seq_size = (query.shape[0], query.shape[1])
    length = keys.shape[1]
    query_heads = query.reshape(seq_number, seq_size, -1, HD)
    key_heads = keys.reshape(seq_number, length, -1, HD)
    scores = jnp.einsum(
        "cqhd,ckhd->chqk", query_heads, key_heads, preferred_element_type=jnp.float32
    ) * HD ** (-0.5)
    allowed = jnp.arange(length)[None, :] <= (first_pos + jnp.arange(seq_size))[:, None]
    return (jnp.where(allowed[None, None], scores, -1e30), query_heads, key_heads)


def attend_forward(query, keys, values, first_pos):
    seq_number, seq_size = (query.shape[0], query.shape[1])
    scores, query_heads, key_heads = masked_scores(query, keys, first_pos)
    largest = jnp.max(scores, axis=-1, keepdims=True)
    raised = jnp.exp(scores - largest)
    total = jnp.sum(raised, axis=-1, keepdims=True)
    probs = (raised / total).astype(jnp.bfloat16)
    value_heads = values.reshape(seq_number, values.shape[1], -1, HD)
    mixed = jnp.einsum("chqk,ckhd->cqhd", probs, value_heads, preferred_element_type=jnp.float32)
    return (mixed.reshape(seq_number, seq_size, -1), largest + jnp.log(total))


def attend_backward(query, keys, values, grad_mixed, log_total, first_pos):
    seq_number, seq_size = (query.shape[0], query.shape[1])
    length = keys.shape[1]
    scores, query_heads, key_heads = masked_scores(query, keys, first_pos)
    probs = jnp.exp(scores - log_total)
    value_heads = values.reshape(seq_number, length, -1, HD)
    grad_heads = grad_mixed.reshape(seq_number, seq_size, -1, HD)
    grad_probs = jnp.einsum(
        "cqhd,ckhd->chqk", grad_heads, value_heads, preferred_element_type=jnp.float32
    )
    delta = jnp.sum(probs * grad_probs, axis=-1)
    grad_scores = (probs * (grad_probs - delta[..., None])).astype(jnp.bfloat16)
    grad_query = jnp.einsum(
        "chqk,ckhd->cqhd", grad_scores, key_heads, preferred_element_type=jnp.float32
    ) * HD ** (-0.5)
    grad_query = grad_query.reshape(seq_number, seq_size, -1)
    return (grad_query, delta)


def attend_key_side(query_all, keys, values, grad_all, total_all, delta_all, key_first):
    seq_number, length = (query_all.shape[0], query_all.shape[1])
    key_count = keys.shape[1]
    query_heads = query_all.reshape(seq_number, length, -1, HD)
    key_heads = keys.reshape(seq_number, key_count, -1, HD)
    value_heads = values.reshape(seq_number, key_count, -1, HD)
    grad_heads = grad_all.reshape(seq_number, length, -1, HD)
    scores = jnp.einsum(
        "cqhd,ckhd->chqk", query_heads, key_heads, preferred_element_type=jnp.float32
    ) * HD ** (-0.5)
    allowed = (key_first + jnp.arange(key_count))[None, :] <= jnp.arange(length)[:, None]
    scores = jnp.where(allowed[None, None], scores, -1e30)
    probs = jnp.exp(scores - total_all[..., None])
    probs_low = probs.astype(jnp.bfloat16)
    grad_probs = jnp.einsum(
        "cqhd,ckhd->chqk", grad_heads, value_heads, preferred_element_type=jnp.float32
    )
    grad_scores = (probs * (grad_probs - delta_all[..., None])).astype(jnp.bfloat16)
    grad_values = jnp.einsum(
        "chqk,cqhd->ckhd", probs_low, grad_heads, preferred_element_type=jnp.float32
    )
    grad_keys = jnp.einsum(
        "chqk,cqhd->ckhd", grad_scores, query_heads, preferred_element_type=jnp.float32
    ) * HD ** (-0.5)
    return (
        grad_keys.reshape(seq_number, key_count, -1),
        grad_values.reshape(seq_number, key_count, -1),
    )


def local(
    tokens,
    w_qkv,
    w_out,
    w_up,
    w_down,
    gain_attn,
    gain_ffn,
    w_router,
    head_quarters,
    ffn_quarters,
    router_targets,
    cotangent,
):
    row_count = tokens.shape[0]
    seq_rank = lax.axis_index("seq")
    seq_count = lax.axis_size("seq")
    head_rank = lax.axis_index("heads")
    head_width = w_out.shape[0]
    ffn_width = w_up.shape[1]
    short_rows = NSHORT * SHORT_DEV
    column = jnp.arange(row_count)
    is_short = column < short_rows
    offset = column - short_rows
    seq_id = jnp.where(is_short, column // SHORT_DEV, NSHORT + offset // (2 * SHORT_DEV))
    position = jnp.where(
        is_short,
        seq_rank * SHORT_DEV + column % SHORT_DEV,
        seq_rank * 2 * SHORT_DEV + offset % (2 * SHORT_DEV),
    )
    in_seq = seq_id[:, None] == jnp.arange(SEQS)[None, :]
    member = in_seq.astype(jnp.float32)
    seq_length = jnp.where(
        jnp.arange(SEQS) < NSHORT, SHORT_DEV * seq_count, 2 * SHORT_DEV * seq_count
    ).astype(jnp.float32)
    head_level = jnp.sum(jnp.where(in_seq, head_quarters[None, :], 0), axis=1)
    ffn_level = jnp.sum(jnp.where(in_seq, ffn_quarters[None, :], 0), axis=1)
    head_index = head_rank * (head_width // HD) + jnp.arange(head_width) // HD
    head_live = (head_index[None, :] < (head_level * (H // LEVELS))[:, None]).astype(jnp.bfloat16)
    unit_index = head_rank * ffn_width + jnp.arange(ffn_width)
    ffn_live = (unit_index[None, :] < (ffn_level * (FF // LEVELS))[:, None]).astype(jnp.float32)
    half_dim = HD // 2
    frequency = 10000.0 ** (-jnp.arange(half_dim, dtype=jnp.float32) * 2.0 / HD)
    angle = position.astype(jnp.float32)[:, None] * frequency[None, :]
    cosine = jnp.cos(angle)[:, None, :]
    sine = jnp.sin(angle)[:, None, :]
    tokens_wide = tokens.astype(jnp.float32)
    hat_one, inverse_one = normalize_parts(tokens_wide)
    normed_one = hat_one * gain_attn
    normed_low = normed_one.astype(jnp.bfloat16)
    flat_qkv = w_qkv.reshape(D, -1)
    projected = jnp.dot(normed_low, flat_qkv, preferred_element_type=jnp.float32).reshape(
        row_count, 3, head_width
    )
    query = rotate(projected[:, 0], cosine, sine, False).astype(jnp.bfloat16)
    keys = rotate(projected[:, 1], cosine, sine, False).astype(jnp.bfloat16)
    values = projected[:, 2].astype(jnp.bfloat16)
    partial_pool = jnp.dot(
        member.T, normed_one, precision=highest, preferred_element_type=jnp.float32
    )
    pooled = (
        lax.psum(partial_pool.astype(jnp.bfloat16), "seq").astype(jnp.float32)
        * lax.rsqrt(seq_length)[:, None]
    )
    shape_list = ((0, NSHORT, SHORT_DEV), (short_rows, NLONG, 2 * SHORT_DEV))
    saved_parts = []
    mixed_parts = []
    for row_start, seq_number, seq_size in shape_list:
        row_stop = row_start + seq_number * seq_size
        piece_query = query[row_start:row_stop].reshape(seq_number, seq_size, head_width)
        piece_keys = keys[row_start:row_stop].reshape(seq_number, seq_size, head_width)
        piece_values = values[row_start:row_stop].reshape(seq_number, seq_size, head_width)
        gathered_keys, gathered_values = gather_rows(piece_keys, piece_values)
        mixed, log_total = attend_forward(
            piece_query, gathered_keys, gathered_values, seq_rank * seq_size
        )
        saved_parts.append(
            (piece_query, piece_keys, piece_values, gathered_keys, gathered_values, log_total)
        )
        mixed_parts.append(mixed.reshape(seq_number * seq_size, head_width))
    heads_out = (jnp.concatenate(mixed_parts, axis=0) * head_live).astype(jnp.bfloat16)
    attn_part = jnp.dot(heads_out, w_out, preferred_element_type=jnp.float32)
    hidden = tokens_wide + lax.psum(attn_part, "heads")
    hat_two, inverse_two = normalize_parts(hidden)
    normed_two = (hat_two * gain_ffn).astype(jnp.bfloat16)
    full_up, full_down = (
        lax.all_gather(w_up, "seq", axis=0, tiled=True),
        lax.all_gather(w_down, "seq", axis=1, tiled=True),
    )
    upward = jnp.dot(normed_two, full_up, preferred_element_type=jnp.float32)
    active = (jnp.square(jnp.maximum(upward, 0.0)) * ffn_live).astype(jnp.bfloat16)
    ffn_part = jnp.dot(active, full_down, preferred_element_type=jnp.float32)
    output = (hidden + lax.psum(ffn_part.astype(jnp.bfloat16), "heads").astype(jnp.float32)).astype(
        jnp.bfloat16
    )
    back_up, back_down = (
        lax.all_gather(w_up, "seq", axis=0, tiled=True),
        lax.all_gather(w_down, "seq", axis=1, tiled=True),
    )
    upward_again = jnp.dot(normed_two, back_up, preferred_element_type=jnp.float32)
    active_again = (jnp.square(jnp.maximum(upward_again, 0.0)) * ffn_live).astype(jnp.bfloat16)
    grad_active = jnp.dot(cotangent, back_down.T, preferred_element_type=jnp.float32).astype(
        jnp.bfloat16
    )
    grad_upward = (
        grad_active.astype(jnp.float32) * ffn_live * 2.0 * jnp.maximum(upward_again, 0.0)
    ).astype(jnp.bfloat16)
    grad_down_part = jnp.dot(active_again.T, cotangent, preferred_element_type=jnp.float32)
    grad_up_part = jnp.dot(normed_two.T, grad_upward, preferred_element_type=jnp.float32)
    grad_two = lax.psum(
        jnp.dot(grad_upward, back_up.T, preferred_element_type=jnp.float32), "heads"
    )
    grad_up, grad_down = (
        lax.psum_scatter(
            grad_up_part.astype(jnp.bfloat16), "seq", scatter_dimension=0, tiled=True
        ).astype(jnp.float32),
        lax.psum_scatter(
            grad_down_part.astype(jnp.bfloat16), "seq", scatter_dimension=1, tiled=True
        ).astype(jnp.float32),
    )
    back_two, grad_gain_two = normalize_back(grad_two, hat_two, inverse_two, gain_ffn)
    grad_hidden = cotangent.astype(jnp.float32) + back_two
    grad_attn = grad_hidden.astype(jnp.bfloat16)
    grad_out_part = jnp.dot(heads_out.T, grad_attn, preferred_element_type=jnp.float32)
    grad_heads = (
        jnp.dot(grad_attn, w_out.T, preferred_element_type=jnp.float32).astype(jnp.bfloat16)
        * head_live
    )
    query_grads = []
    key_grads = []
    value_grads = []
    for shape_entry, saved in zip(shape_list, saved_parts):
        row_start, seq_number, seq_size = shape_entry
        piece_query, piece_keys, piece_values, gathered_keys, gathered_values, log_total = saved
        piece_grad = grad_heads[row_start : row_start + seq_number * seq_size].reshape(
            seq_number, seq_size, head_width
        )
        grad_query, delta = attend_backward(
            piece_query, gathered_keys, gathered_values, piece_grad, log_total, seq_rank * seq_size
        )
        query_all, grad_all = (
            lax.all_gather(piece_query, "seq", axis=1, tiled=True),
            lax.all_gather(piece_grad, "seq", axis=1, tiled=True),
        )
        total_all, delta_all = (
            lax.all_gather(log_total[..., 0], "seq", axis=2, tiled=True),
            lax.all_gather(delta, "seq", axis=2, tiled=True),
        )
        local_keys, local_values = attend_key_side(
            query_all, piece_keys, piece_values, grad_all, total_all, delta_all, seq_rank * seq_size
        )
        query_grads.append(grad_query.reshape(seq_number * seq_size, head_width))
        key_grads.append(local_keys.reshape(seq_number * seq_size, head_width))
        value_grads.append(local_values.reshape(seq_number * seq_size, head_width))
    grad_query_all = rotate(jnp.concatenate(query_grads, axis=0), cosine, sine, True)
    grad_key_all = rotate(jnp.concatenate(key_grads, axis=0), cosine, sine, True)
    grad_value_all = jnp.concatenate(value_grads, axis=0)
    grad_projected = (
        jnp.stack([grad_query_all, grad_key_all, grad_value_all], axis=1)
        .astype(jnp.bfloat16)
        .reshape(row_count, -1)
    )
    grad_qkv_part = jnp.dot(
        normed_low.T, grad_projected, preferred_element_type=jnp.float32
    ).reshape(D, 3, head_width)
    grad_one = lax.psum(
        jnp.dot(grad_projected, flat_qkv.T, preferred_element_type=jnp.float32).astype(
            jnp.bfloat16
        ),
        "heads",
    ).astype(jnp.float32)
    logits = jnp.dot(pooled, w_router, precision=highest, preferred_element_type=jnp.float32)
    logit_grads = []
    for group in range(2):
        group_logits = logits[:, LEVELS * group : LEVELS * (group + 1)]
        raised = jnp.exp(group_logits - jnp.max(group_logits, axis=1, keepdims=True))
        chosen = (jnp.arange(LEVELS)[None, :] == router_targets[:, group][:, None]).astype(
            jnp.float32
        )
        logit_grads.append(raised / jnp.sum(raised, axis=1, keepdims=True) - chosen)
    grad_logits = jnp.concatenate(logit_grads, axis=1)
    grad_router = jnp.dot(
        pooled.T, grad_logits, precision=highest, preferred_element_type=jnp.float32
    )
    grad_pooled = (
        jnp.dot(grad_logits, w_router.T, precision=highest, preferred_element_type=jnp.float32)
        * lax.rsqrt(seq_length)[:, None]
    )
    grad_one = grad_one + jnp.dot(
        member, grad_pooled, precision=highest, preferred_element_type=jnp.float32
    )
    back_one, grad_gain_one = normalize_back(grad_one, hat_one, inverse_one, gain_attn)
    grad_tokens = grad_hidden + back_one
    grad_qkv, grad_out, grad_gain_attn, grad_gain_ffn = (
        lax.psum(grad_qkv_part.astype(jnp.bfloat16), "seq").astype(jnp.float32),
        lax.psum(grad_out_part.astype(jnp.bfloat16), "seq").astype(jnp.float32),
        lax.psum(grad_gain_one.astype(jnp.bfloat16), "seq").astype(jnp.float32),
        lax.psum(grad_gain_two.astype(jnp.bfloat16), "seq").astype(jnp.float32),
    )
    return (
        output,
        grad_tokens,
        grad_qkv,
        grad_out,
        grad_up,
        grad_down,
        grad_gain_attn,
        grad_gain_ffn,
        grad_router,
    )


def solution(mesh):
    return jax.shard_map(
        local,
        mesh=mesh,
        in_specs=(
            P("seq", None),
            P(None, None, "heads"),
            P("heads", None),
            P("seq", "heads"),
            P("heads", "seq"),
            P(),
            P(),
            P(),
            P(),
            P(),
            P(),
            P("seq", None),
        ),
        out_specs=(
            P("seq", None),
            P("seq", None),
            P(None, None, "heads"),
            P("heads", None),
            P("seq", "heads"),
            P("heads", "seq"),
            P(),
            P(),
            P(),
        ),
        check_vma=False,
    )
```

profile of v0, /device:TPU:0, one launch (start us, length us, event | category | flops | bytes accessed | tf_op | source)
XLA Modules:
  0.0 1484.3 jit_solution(1231842556310068782)
XLA Ops:
  21.9 11.1 fusion.159
  81.1 34.7 %all-gather.13.cloned.1.call-done = bf16[3,1024,512]{2,1,0:T(8,128)(2,1)} async-done(((bf16[3,128,512]{2,1,0:T(8,128)(2,1)}), bf16[3,1024,512]{2,1,0:T(8,128)(2,1)}) %all-gather.13.cloned.1.call-update) | async-done | bytes 3145744 | tf_op jit(solution)/shard_map/all_gather | solution.py:50
  134.2 29.5 %all-gather.17.cloned.1.call-done = bf16[2,2048,512]{2,1,0:T(8,128)(2,1)} async-done(((bf16[2,256,512]{2,1,0:T(8,128)(2,1)}), bf16[2,2048,512]{2,1,0:T(8,128)(2,1)}) %all-gather.17.cloned.1.call-update) | async-done | bytes 4194320 | tf_op jit(solution)/shard_map/all_gather | solution.py:50
  185.6 25.3 %all-gather.15.cloned.1.call-done = bf16[2,2048,512]{2,1,0:T(8,128)(2,1)} async-done(((bf16[2,256,512]{2,1,0:T(8,128)(2,1)}), bf16[2,2048,512]{2,1,0:T(8,128)(2,1)}) %all-gather.15.cloned.1.call-update) | async-done | bytes 4194320 | tf_op jit(solution)/shard_map/all_gather | solution.py:51
  217.1 11.0 fusion.70
  240.7 153.0 %all-reduce.8.cloned.1.call-done = f32[896,2048]{1,0:T(8,128)} async-done(((f32[896,2048]{1,0:T(8,128)}), f32[896,2048]{1,0:T(8,128)}) %all-reduce.8.cloned.1.call-update) | async-done | bytes 7340048 | tf_op jit(solution)/shard_map/psum | solution.py:210
  402.5 74.7 %all-gather.19.cloned.1.call-done = bf16[2048,2048]{1,0:T(8,128)(2,1)} async-done(((bf16[256,2048]{1,0:T(8,128)(2,1)}), bf16[2048,2048]{1,0:T(8,128)(2,1)}) %all-gather.19.cloned.1.call-update) | async-done | bytes 8388624 | tf_op jit(solution)/shard_map/all_gather | solution.py:214
  477.2 14.6 fusion.154
  491.8 67.9 %all-gather.21.cloned.1.call-done = bf16[2048,2048]{1,0:T(8,128)(2,1)} async-done(((bf16[2048,256]{1,0:T(8,128)(2,1)}), bf16[2048,2048]{1,0:T(8,128)(2,1)}) %all-gather.21.cloned.1.call-update) | async-done | bytes 8388624 | tf_op jit(solution)/shard_map/all_gather | solution.py:215
  559.8 15.0 %fusion.29 = bf16[896,2048]{1,0:T(8,128)(2,1)} fusion(f32[896,2048]{1,0:T(8,128)} %fusion.154, s32[2048]{0:T(1024)S(1)} %iota_add_fusion, s32[896]{0:T(1024)S(1)} %broadcast_multiply_fusion, bf16[896,2048]{1,0:T(8,128)(2,1)} %param.23, bf16[2048,2048]{1,0:T(8,128)(2,1)} %all-gather.21.cloned.1.call-done), kind=kOutput, calls=%fused_computation.42 | convolution fusion | flops 7530872832 | bytes 23080448 | tf_op jit(solution)/shard_map/dot_general | solution.py:229
  574.7 11.3 fusion.160
  593.4 146.5 %all-reduce.10.cloned.1.call-done = f32[896,2048]{1,0:T(8,128)} async-done(((f32[896,2048]{1,0:T(8,128)}), f32[896,2048]{1,0:T(8,128)}) %all-reduce.10.cloned.1.call-update) | async-done | bytes 7340048 | tf_op jit(solution)/shard_map/psum | solution.py:237
  760.6 15.4 %convolution_convert_fusion = bf16[2048,2048]{1,0:T(8,128)(2,1)} fusion(bf16[896,2048]{1,0:T(8,128)(2,1)} %param.23, f32[896,2048]{1,0:T(8,128)} %fusion.154, s32[2048]{0:T(1024)S(1)} %copy-done.58, s32[896]{0:T(1024)S(1)} %copy-done.63), kind=kOutput, calls=%fused_computation.31 | convolution fusion | flops 7529562112 | bytes 19410432 | tf_op jit(solution)/shard_map/dot_general | solution.py:235
  776.1 15.1 %convolution_convert_fusion.1 = bf16[2048,2048]{1,0:T(8,128)(2,1)} fusion(bf16[896,2048]{1,0:T(8,128)(2,1)} %fusion.29, f32[896,2048]{1,0:T(8,128)} %copy-done.3, f32[2048]{0:T(1024)S(1)} %copy-done.45, f32[896]{0:T(1024)S(1)} %add_rsqrt_fusion, f32[896]{0:T(1024)S(1)} %broadcast_multiply_fusion.6), kind=kOutput, calls=%fused_computation.32 | convolution fusion | flops 7527727104 | bytes 19414016 | tf_op jit(solution)/shard_map/dot_general | solution.py:236
  799.9 14.7 all_gather.51
  833.7 15.8 %all_gather.55 = f32[2,4,2048]{2,1,0:T(4,128)} all-gather(f32[2,4,256]{2,1,0:T(4,128)S(1)} %bitcast.162), channel_id=1, replica_groups=mesh['heads'=4,'seq'=8] {'seq'}, dimensions={2}, use_global_device_ids=true | all-gather | bytes 73728 | tf_op jit(solution)/shard_map/all_gather | solution.py:273
  849.4 10.4 fusion.87
  872.7 13.8 multiply_reduce_fusion
  886.5 14.8 fusion.74
  901.6 15.1 %all_gather.53 = f32[3,4,1024]{2,1,0:T(4,128)S(1)} all-gather(f32[3,4,128]{2,1,0:T(4,128)S(1)} %get-tuple-element.61), channel_id=1, replica_groups=mesh['heads'=4,'seq'=8] {'seq'}, dimensions={2}, use_global_device_ids=true | all-gather | bytes 55296 | tf_op jit(solution)/shard_map/all_gather | solution.py:274
  916.7 15.4 %all_gather.57 = f32[2,4,2048]{2,1,0:T(4,128)} all-gather(f32[2,4,256]{2,1,0:T(4,128)S(1)} %get-tuple-element.59), channel_id=1, replica_groups=mesh['heads'=4,'seq'=8] {'seq'}, dimensions={2}, use_global_device_ids=true | all-gather | bytes 73728 | tf_op jit(solution)/shard_map/all_gather | solution.py:274
  956.0 9.5 fusion.67
  966.0 13.0 fusion.72
  997.4 12.3 convolution_convert_fusion.2
  1010.4 15.1 %convolution_convert_fusion.3 = bf16[896,2048]{1,0:T(8,128)(2,1)} fusion(bf16[2048,2048]{1,0:T(8,128)(2,1)} %all-gather.21.cloned.1.call-done, f32[896,2048]{1,0:T(8,128)} %fusion.154, s32[2048]{0:T(1024)S(1)} %copy-done.59, s32[896]{0:T(1024)S(1)} %copy-done.64), kind=kOutput, calls=%fused_computation.73 | convolution fusion | flops 7527202816 | bytes 19410432 | tf_op jit(solution)/shard_map/dot_general | solution.py:219
  1025.5 10.2 bitcast_convert_fusion
  1041.9 28.2 %psum.67 = bf16[5,2048]{1,0:T(8,128)(2,1)S(1)} all-reduce(bf16[5,2048]{1,0:T(8,128)(2,1)S(1)} %fusion.55), channel_id=1, replica_groups=mesh['heads'=4,'seq'=8] {'seq'}, use_global_device_ids=true, to_apply=%region_18.19 | all-reduce | flops 10240 | bytes 40960 | tf_op jit(solution)/shard_map/psum | solution.py:189
  1074.9 22.1 %reduce-scatter.3.cloned.1.call-done = bf16[256,2048]{1,0:T(8,128)(2,1)} async-done(((bf16[2048,2048]{1,0:T(8,128)(2,1)}), bf16[256,2048]{1,0:T(8,128)(2,1)}) %reduce-scatter.3.cloned.1.call-update) | async-done | bytes 1048592 | tf_op jit(solution)/shard_map/reduce_scatter | solution.py:241
  1099.8 173.5 %all-reduce.12.cloned.1.call-done = (bf16[2048,3,512]{2,0,1:T(8,128)(2,1)}, bf16[512,2048]{1,0:T(8,128)(2,1)}) async-done(((bf16[2048,3,512]{2,0,1:T(8,128)(2,1)}, bf16[512,2048]{1,0:T(8,128)(2,1)}), (bf16[2048,3,512]{2,0,1:T(8,128)(2,1)}, bf16[512,2048]{1,0:T(8,128)(2,1)})) %all-reduce.12.cloned.1.call-update) | async-done | bytes 8388624 | tf_op jit(solution)/shard_map/psum | solution.py:322
  1284.8 148.0 %all-reduce.14.cloned.1.call-done = (bf16[896,2048]{1,0:T(8,128)(2,1)}, bf16[896,2048]{1,0:T(8,128)(2,1)}) async-done(((bf16[896,2048]{1,0:T(8,128)(2,1)}, bf16[896,2048]{1,0:T(8,128)(2,1)}), (bf16[896,2048]{1,0:T(8,128)(2,1)}, bf16[896,2048]{1,0:T(8,128)(2,1)})) %all-reduce.14.cloned.1.call-update) | async-done | bytes 7340048 | tf_op jit(solution)/shard_map/psum | solution.py:220
  1449.5 16.5 %all-reduce = (bf16[2048]{0:T(1024)(128)(2,1)S(1)}, bf16[2048]{0:T(1024)(128)(2,1)S(1)}) all-reduce(bf16[2048]{0:T(1024)(128)(2,1)S(1)} %get-tuple-element.11, bf16[2048]{0:T(1024)(128)(2,1)S(1)} %copy-done.52), channel_id=1, replica_groups=mesh['heads'=4,'seq'=8] {'seq'}, use_global_device_ids=true, to_apply=%region_30.31 | all-reduce | flops 4096 | bytes 16384 | tf_op jit(solution)/shard_map/psum | solution.py:324
  1467.2 10.4 fusion.23
  (303 shorter events, 285.4 us)
Async XLA Ops:
  7.2 225.8 %copy-start = (bf16[512,2048]{1,0:T(8,128)(2,1)S(1)}, bf16[512,2048]{1,0:T(8,128)(2,1)}, u32[]{:S(2)}) copy-start(bf16[512,2048]{1,0:T(8,128)(2,1)} %param.14) | copy-start | bytes 6291460
  7.2 69.3 %all-gather.11.cloned.1.call-start = ((), (), s32[]{:S(2)}) async-start(), calls=%async_computation.2 | async-start | bytes 3538944 | tf_op jit(solution)/shard_map/all_gather | solution.py:51
  35.4 80.4 %all-gather.13.cloned.1.call-start = ((), (), s32[]{:S(2)}) async-start(), calls=%async_computation.3 | async-start | bytes 3538944 | tf_op jit(solution)/shard_map/all_gather | solution.py:50
  57.9 105.9 %all-gather.17.cloned.1.call-start = ((), (), s32[]{:S(2)}) async-start(), calls=%async_computation.5 | async-start | bytes 4718592 | tf_op jit(solution)/shard_map/all_gather | solution.py:50
  61.7 149.3 %all-gather.15.cloned.1.call-start = ((), (), s32[]{:S(2)}) async-start(), calls=%async_computation.4 | async-start | bytes 4718592 | tf_op jit(solution)/shard_map/all_gather | solution.py:51
  63.6 330.0 %all-reduce.8.cloned.1.call-start = ((), (), s32[]{:S(2)}) async-start(), calls=%async_computation.6 | async-start | bytes 14680064 | tf_op jit(solution)/shard_map/psum | solution.py:210
  63.9 56.5 %copy-start.60 = (s32[256]{0:T(256)}, s32[256]{0:T(256)S(1)}, u32[]{:S(2)}) copy-start(s32[256]{0:T(256)S(1)} %iota_add_fusion.2) | copy-start | bytes 3076
  63.9 168.0 %copy-start.69 = (s32[512]{0:T(512)}, s32[512]{0:T(512)S(1)}, u32[]{:S(2)}) copy-start(s32[512]{0:T(512)S(1)} %fusion.125) | copy-start | bytes 6148
  68.7 163.3 %copy-start.65 = (s32[896]{0:T(1024)}, s32[896]{0:T(1024)S(1)}, u32[]{:S(2)}) copy-start(s32[896]{0:T(1024)S(1)} %broadcast_multiply_fusion.1) | copy-start | bytes 10756
  68.8 57.0 %copy-start.11 = (pred[128,1024]{1,0:T(8,128)(4,1)}, pred[128,1024]{1,0:T(8,128)(4,1)S(1)}, u32[]{:S(2)}) copy-start(pred[128,1024]{1,0:T(8,128)(4,1)S(1)} %iota_compare_fusion.3) | copy-start | bytes 393220
  185.6 42.5 %copy-start.46 = (f32[2,4,256]{2,1,0:T(4,128)}, f32[2,4,256]{2,1,0:T(4,128)S(1)}, u32[]{:S(2)}) copy-start(f32[2,4,256]{2,1,0:T(4,128)S(1)} %fusion) | copy-start | bytes 24580
  239.3 237.9 %all-gather.19.cloned.1.call-start = ((), (), s32[]{:S(2)}) async-start(), calls=%async_computation.7 | async-start | bytes 9437184 | tf_op jit(solution)/shard_map/all_gather | solution.py:214
  239.8 319.9 %all-gather.21.cloned.1.call-start = ((), (), s32[]{:S(2)}) async-start(), calls=%async_computation.8 | async-start | bytes 9437184 | tf_op jit(solution)/shard_map/all_gather | solution.py:215
  240.6 499.3 %all-reduce.10.cloned.1.call-start = ((), (), s32[]{:S(2)}) async-start(), calls=%async_computation.9 | async-start | bytes 14680064 | tf_op jit(solution)/shard_map/psum | solution.py:237
  240.7 319.1 %copy-start.57 = (s32[2048]{0:T(1024)}, s32[2048]{0:T(1024)S(1)}, u32[]{:S(2)}) copy-start(s32[2048]{0:T(1024)S(1)} %iota_add_fusion) | copy-start | bytes 24580
  240.7 319.1 %copy-start.62 = (s32[896]{0:T(1024)}, s32[896]{0:T(1024)S(1)}, u32[]{:S(2)}) copy-start(s32[896]{0:T(1024)S(1)} %broadcast_multiply_fusion) | copy-start | bytes 10756
  398.6 78.6 %copy-start.44 = (f32[2048]{0:T(1024)S(1)}, f32[2048]{0:T(1024)}, u32[]{:S(2)}) copy-start(f32[2048]{0:T(1024)} %param.18) | copy-start | bytes 24580
  586.1 209.2 %all-gather.23.cloned.1.call-start = ((), (), s32[]{:S(2)}) async-start(), calls=%async_computation.10 | async-start | bytes 3538944 | tf_op jit(solution)/shard_map/all_gather | solution.py:269
  590.0 237.3 %all-gather.27.cloned.1.call-start = ((), (), s32[]{:S(2)}) async-start(), calls=%async_computation.12 | async-start | bytes 4718592 | tf_op jit(solution)/shard_map/all_gather | solution.py:269
  593.3 154.0 %copy-start.45 = (f32[2048]{0:T(1024)S(1)}, f32[2048]{0:T(1024)}, u32[]{:S(2)}) copy-start(f32[2048]{0:T(1024)} %param.18) | copy-start | bytes 24580
  593.3 346.1 %all-gather.25.cloned.1.call-start = ((), (), s32[]{:S(2)}) async-start(), calls=%async_computation.11 | async-start | bytes 3538944 | tf_op jit(solution)/shard_map/all_gather | solution.py:270
  758.4 197.6 %all-gather.29.cloned.1.call-start = ((), (), s32[]{:S(2)}) async-start(), calls=%async_computation.13 | async-start | bytes 4718592 | tf_op jit(solution)/shard_map/all_gather | solution.py:270
  760.6 311.6 %reduce-scatter.5.cloned.1.call-start = ((), (), s32[]{:S(2)}) async-start(), calls=%async_computation.15 | async-start | bytes 9437184 | tf_op jit(solution)/shard_map/reduce_scatter | solution.py:244
  776.1 320.9 %reduce-scatter.3.cloned.1.call-start = ((), (), s32[]{:S(2)}) async-start(), calls=%async_computation.14 | async-start | bytes 9437184 | tf_op jit(solution)/shard_map/reduce_scatter | solution.py:241
  791.3 23.4 %copy-start.20 = (bf16[384,4,128]{2,0,1:T(8,128)(2,1)S(1)}, bf16[384,4,128]{2,0,1:T(8,128)(2,1)}, u32[]{:S(2)}) copy-start(bf16[384,4,128]{2,0,1:T(8,128)(2,1)} %copy-done.19) | copy-start | bytes 1179652
  791.3 482.0 %all-reduce.12.cloned.1.call-start = ((), (), s32[]{:S(2)}) async-start(), calls=%async_computation.16 | async-start | bytes 16777216 | tf_op jit(solution)/shard_map/psum | solution.py:322
  820.3 29.1 %copy-start.18 = (bf16[512,4,128]{2,0,1:T(8,128)(2,1)S(1)}, bf16[512,4,128]{2,0,1:T(8,128)(2,1)}, u32[]{:S(2)}) copy-start(bf16[512,4,128]{2,0,1:T(8,128)(2,1)} %copy-done.17) | copy-start | bytes 1572868
  886.5 45.6 %copy-start.31 = (f32[48,8,4,128]{3,1,2,0:T(8,128)S(1)}, f32[48,8,4,128]{3,1,2,0:T(8,128)}, u32[]{:S(2)}) copy-start(f32[48,8,4,128]{3,1,2,0:T(8,128)} %copy.273) | copy-start | bytes 2359300
  901.6 37.8 %copy-start.41 = (f32[3,4,1024]{2,1,0:T(4,128)S(1)}, f32[3,4,1024]{2,1,0:T(4,128)}, u32[]{:S(2)}) copy-start(f32[3,4,1024]{2,1,0:T(4,128)} %all_gather.51) | copy-start | bytes 147460
  1009.7 423.1 %all-reduce.14.cloned.1.call-start = ((), (), s32[]{:S(2)}) async-start(), calls=%async_computation.17 | async-start | bytes 14680064 | tf_op jit(solution)/shard_map/psum | solution.py:220
  1035.7 34.4 %copy-start.37 = (f32[2048,8]{0,1:T(8,128)S(1)}, f32[2048,8]{0,1:T(8,128)}, u32[]{:S(2)}) copy-start(f32[2048,8]{0,1:T(8,128)} %param.19) | copy-start | bytes 196612
  1035.7 35.1 %copy-start.71 = (s32[5,2]{0,1:T(2,128)S(1)}, s32[5,2]{0,1:T(2,128)}, u32[]{:S(2)}) copy-start(s32[5,2]{0,1:T(2,128)} %param.22) | copy-start | bytes 124
  (58 other events, 343.4 us)
Sparse Core Ops, SparseCore 0:
  35.5 40.9 all-gather.10
  78.6 37.1 all-gather.12
  118.0 45.7 all-gather.16
  165.2 45.6 all-gather.14
  239.4 154.2 all-reduce.7
  395.1 82.0 all-gather.18
  478.7 80.9 all-gather.20
  586.2 153.6 all-reduce.9
  741.5 38.1 all-gather.22
  781.2 46.1 all-gather.26
  829.0 40.0 all-gather.24
  871.1 44.4 all-gather.28
  917.9 87.9 reduce-scatter.4
  1008.6 88.2 reduce-scatter.2
  1099.2 174.0 all-reduce.11
  1277.2 155.5 all-reduce.13
where the time goes:
time: 1490 us; the launch traced here: 1480 us
  waiting for transfers between devices  891 us (60%)
  matrix products  268 us (18%)
  local copies, waits for them, and re-layouts  115 us (8%)
  blocking collectives  106 us (7%)
  other arithmetic  88.5 us (6%)
  between operations  15.1 us (1%)
    psum x1, waiting for transfers between devices, local(): lax.psum(grad_qkv_part.astype(jnp.bfloat16), 'seq').astype(jnp.float32)  174 us
    psum x1, waiting for transfers between devices, local(): hidden = tokens_wide + lax.psum(attn_part, 'heads')  153 us
    psum x1, waiting for transfers between devices, local(): lax.psum(ffn_part.astype(jnp.bfloat16), 'heads').astype(jnp.float32)  148 us
    psum x1, waiting for transfers between devices, local(): lax.psum(jnp.dot(grad_upward, back_up.T, preferred_element_type=jnp.float...  146 us
    all_gather x1, waiting for transfers between devices, local(): lax.all_gather(w_up, 'seq', axis=0, tiled=True)  74.7 us
    all_gather x1, waiting for transfers between devices, local(): lax.all_gather(w_down, 'seq', axis=1, tiled=True)  67.9 us
    all_gather x2, waiting for transfers between devices, gather_rows(): lax.all_gather(keys, 'seq', axis=1, tiled=True)  64.2 us
    unnamed x153, local copies, waits for them, and re-layouts  34.3 us
  transfers between devices with their start and end apart: 16, of which 12 were waited for; matrix products, arithmetic and copies ran while one was open for 23% of the time, Pallas kernels for 0%

commit v1 on v0

--- a/solution.py
+++ b/solution.py
@@ -319,7 +319,9 @@
     back_one, grad_gain_one = normalize_back(grad_one, hat_one, inverse_one, gain_attn)
     grad_tokens = grad_hidden + back_one
     grad_qkv, grad_out, grad_gain_attn, grad_gain_ffn = (
-        lax.psum(grad_qkv_part.astype(jnp.bfloat16), "seq").astype(jnp.float32),
+        jnp.sum(lax.all_gather(grad_qkv_part.astype(jnp.bfloat16), "seq"), axis=0).astype(
+            jnp.float32
+        ),
         lax.psum(grad_out_part.astype(jnp.bfloat16), "seq").astype(jnp.float32),
         lax.psum(grad_gain_one.astype(jnp.bfloat16), "seq").astype(jnp.float32),
         lax.psum(grad_gain_two.astype(jnp.bfloat16), "seq").astype(jnp.float32),

time: 1490 us -> 1790 us (1.20)
  waiting for transfers between devices: 891 us -> 1180 us
  other arithmetic: 88.5 us -> 108 us
    all_gather x0 -> x1, waiting for transfers between devices: none -> 385 us  [local(): lax.all_gather(grad_qkv_part.astype(jnp.bfloat16), 'seq')]
    psum x1, waiting for transfers between devices: 174 us -> 0.02 us  [local(): lax.psum(grad_out_part.astype(jnp.bfloat16), 'seq').astype(jnp.float32)]
    reduce_scatter x1, waiting for transfers between devices: 22.1 us -> 88 us  [local(): lax.psum_scatter(grad_up_part.astype(jnp.bfloat16), 'seq', scatter_dimens...]
    reduce_sum x0 -> x1, other arithmetic: none -> 20 us  [local(): jnp.sum(lax.all_gather(grad_qkv_part.astype(jnp.bfloat16), 'seq'), axis=0)]
    unnamed x153 -> x151, local copies, waits for them, and re-layouts: 34.3 us -> 35.8 us
  transfers between devices with their start and end apart: 16 -> 17, of which waited for: 12 -> 13; matrix products, arithmetic and copies ran while one was open for 23% -> 20% of each run, Pallas kernels for 0% -> 0%
where the time goes in v1:
time: 1790 us
  waiting for transfers between devices  1180 us (66%)
  matrix products  268 us (15%)
  local copies, waits for them, and re-layouts  113 us (6%)
  other arithmetic  108 us (6%)
  blocking collectives  105 us (6%)
    all_gather x1, waiting for transfers between devices, local(): lax.all_gather(grad_qkv_part.astype(jnp.bfloat16), 'seq')  385 us
    psum x1, waiting for transfers between devices, local(): lax.psum(ffn_part.astype(jnp.bfloat16), 'heads').astype(jnp.float32)  155 us
    psum x1, waiting for transfers between devices, local(): hidden = tokens_wide + lax.psum(attn_part, 'heads')  153 us
    psum x1, waiting for transfers between devices, local(): lax.psum(jnp.dot(grad_upward, back_up.T, preferred_element_type=jnp.float...  150 us
    reduce_scatter x1, waiting for transfers between devices, local(): lax.psum_scatter(grad_up_part.astype(jnp.bfloat16), 'seq', scatter_dimens...  88 us
    all_gather x1, waiting for transfers between devices, local(): lax.all_gather(w_up, 'seq', axis=0, tiled=True)  74.7 us
    all_gather x1, waiting for transfers between devices, local(): lax.all_gather(w_down, 'seq', axis=1, tiled=True)  68.1 us
    all_gather x2, waiting for transfers between devices, gather_rows(): lax.all_gather(keys, 'seq', axis=1, tiled=True)  64 us
  transfers between devices with their start and end apart: 17, of which 13 were waited for; matrix products, arithmetic and copies ran while one was open for 20% of the time, Pallas kernels for 0%

profile of v1, /device:TPU:0, one launch (start us, length us, event | category | flops | bytes accessed | tf_op | source)
XLA Modules:
  0.0 1787.7 jit_solution(6313281498601690010)
XLA Ops:
  21.9 11.1 fusion.159
  81.2 34.6 %all-gather.15.cloned.1.call-done = bf16[3,1024,512]{2,1,0:T(8,128)(2,1)} async-done(((bf16[3,128,512]{2,1,0:T(8,128)(2,1)}), bf16[3,1024,512]{2,1,0:T(8,128)(2,1)}) %all-gather.15.cloned.1.call-update) | async-done | bytes 3145744 | tf_op jit(solution)/shard_map/all_gather | solution.py:50
  134.4 29.4 %all-gather.19.cloned.1.call-done = bf16[2,2048,512]{2,1,0:T(8,128)(2,1)} async-done(((bf16[2,256,512]{2,1,0:T(8,128)(2,1)}), bf16[2,2048,512]{2,1,0:T(8,128)(2,1)}) %all-gather.19.cloned.1.call-update) | async-done | bytes 4194320 | tf_op jit(solution)/shard_map/all_gather | solution.py:50
  185.7 25.3 %all-gather.17.cloned.1.call-done = bf16[2,2048,512]{2,1,0:T(8,128)(2,1)} async-done(((bf16[2,256,512]{2,1,0:T(8,128)(2,1)}), bf16[2,2048,512]{2,1,0:T(8,128)(2,1)}) %all-gather.17.cloned.1.call-update) | async-done | bytes 4194320 | tf_op jit(solution)/shard_map/all_gather | solution.py:51
  217.1 11.0 fusion.70
  240.7 153.0 %all-reduce.7.cloned.1.call-done = f32[896,2048]{1,0:T(8,128)} async-done(((f32[896,2048]{1,0:T(8,128)}), f32[896,2048]{1,0:T(8,128)}) %all-reduce.7.cloned.1.call-update) | async-done | bytes 7340048 | tf_op jit(solution)/shard_map/psum | solution.py:210
  402.5 74.7 %all-gather.21.cloned.1.call-done = bf16[2048,2048]{1,0:T(8,128)(2,1)} async-done(((bf16[256,2048]{1,0:T(8,128)(2,1)}), bf16[2048,2048]{1,0:T(8,128)(2,1)}) %all-gather.21.cloned.1.call-update) | async-done | bytes 8388624 | tf_op jit(solution)/shard_map/all_gather | solution.py:214
  477.2 14.5 fusion.154
  491.7 68.1 %all-gather.23.cloned.1.call-done = bf16[2048,2048]{1,0:T(8,128)(2,1)} async-done(((bf16[2048,256]{1,0:T(8,128)(2,1)}), bf16[2048,2048]{1,0:T(8,128)(2,1)}) %all-gather.23.cloned.1.call-update) | async-done | bytes 8388624 | tf_op jit(solution)/shard_map/all_gather | solution.py:215
  559.8 15.0 fusion.29
  574.8 11.3 fusion.160
  589.9 150.0 %all-reduce.9.cloned.1.call-done = f32[896,2048]{1,0:T(8,128)} async-done(((f32[896,2048]{1,0:T(8,128)}), f32[896,2048]{1,0:T(8,128)}) %all-reduce.9.cloned.1.call-update) | async-done | bytes 7340048 | tf_op jit(solution)/shard_map/psum | solution.py:237
  768.0 15.6 convolution_convert_fusion
  784.3 15.0 convolution_convert_fusion.1
  807.6 13.8 all_gather.57
  834.1 18.2 %all_gather.61 = f32[2,4,2048]{2,1,0:T(4,128)} all-gather(f32[2,4,256]{2,1,0:T(4,128)S(1)} %bitcast.164), channel_id=1, replica_groups=mesh['heads'=4,'seq'=8] {'seq'}, dimensions={2}, use_global_device_ids=true | all-gather | bytes 73728 | tf_op jit(solution)/shard_map/all_gather | solution.py:273
  852.4 10.3 fusion.87
  862.7 14.0 convolution_convert_fusion.3
  889.0 13.4 multiply_reduce_fusion
  902.4 15.0 fusion.74
  917.7 12.8 all_gather.59
  930.5 15.0 all_gather.63
  972.6 13.6 fusion.72
  998.4 10.2 bitcast_convert_fusion
  1015.1 12.3 convolution_convert_fusion.2
  1033.6 28.2 %psum.60 = bf16[5,2048]{1,0:T(8,128)(2,1)S(1)} all-reduce(bf16[5,2048]{1,0:T(8,128)(2,1)S(1)} %fusion.55), channel_id=1, replica_groups=mesh['heads'=4,'seq'=8] {'seq'}, use_global_device_ids=true, to_apply=%region_18.19 | all-reduce | flops 10240 | bytes 40960 | tf_op jit(solution)/shard_map/psum | solution.py:189
  1076.7 88.0 %reduce-scatter.3.cloned.1.call-done = bf16[256,2048]{1,0:T(8,128)(2,1)} async-done(((bf16[2048,2048]{1,0:T(8,128)(2,1)}), bf16[256,2048]{1,0:T(8,128)(2,1)}) %reduce-scatter.3.cloned.1.call-update) | async-done | bytes 1048592 | tf_op jit(solution)/shard_map/reduce_scatter | solution.py:241
  1167.5 155.1 %all-reduce.13.cloned.1.call-done = (bf16[896,2048]{1,0:T(8,128)(2,1)}, bf16[896,2048]{1,0:T(8,128)(2,1)}) async-done(((bf16[896,2048]{1,0:T(8,128)(2,1)}, bf16[896,2048]{1,0:T(8,128)(2,1)}), (bf16[896,2048]{1,0:T(8,128)(2,1)}, bf16[896,2048]{1,0:T(8,128)(2,1)})) %all-reduce.13.cloned.1.call-update) | async-done | bytes 7340048 | tf_op jit(solution)/shard_map/psum | solution.py:220
  1322.5 10.2 fusion.24
  1332.7 17.2 all-reduce
  1366.6 385.0 %all-gather.33.cloned.1.call-done = bf16[16384,3,512]{2,0,1:T(8,128)(2,1)} async-done(((bf16[2048,3,512]{2,0,1:T(8,128)(2,1)}), bf16[16384,3,512]{2,0,1:T(8,128)(2,1)}) %all-gather.33.cloned.1.call-update) | async-done | bytes 50331664 | tf_op jit(solution)/shard_map/all_gather | solution.py:322
  1751.6 20.0 %reduce_sum.190 = bf16[2048,3,512]{2,0,1:T(8,128)(2,1)} reduce(bf16[8,2048,3,512]{3,1,0,2:T(8,128)(2,1)} %bitcast.129, bf16[]{:T(256)} %constant.126.clone.1), dimensions={0}, to_apply=%region_25.26 | reduce | flops 22020096 | bytes 56623104 | tf_op jit(solution)/shard_map/reduce_sum | solution.py:322
  (305 shorter events, 291.6 us)
Async XLA Ops:
  7.2 225.8 %copy-start = (bf16[512,2048]{1,0:T(8,128)(2,1)S(1)}, bf16[512,2048]{1,0:T(8,128)(2,1)}, u32[]{:S(2)}) copy-start(bf16[512,2048]{1,0:T(8,128)(2,1)} %param.14) | copy-start | bytes 6291460
  7.2 69.3 %all-gather.13.cloned.1.call-start = ((), (), s32[]{:S(2)}) async-start(), calls=%async_computation.2 | async-start | bytes 3538944 | tf_op jit(solution)/shard_map/all_gather | solution.py:51
  35.4 80.4 %all-gather.15.cloned.1.call-start = ((), (), s32[]{:S(2)}) async-start(), calls=%async_computation.3 | async-start | bytes 3538944 | tf_op jit(solution)/shard_map/all_gather | solution.py:50
  57.9 105.9 %all-gather.19.cloned.1.call-start = ((), (), s32[]{:S(2)}) async-start(), calls=%async_computation.5 | async-start | bytes 4718592 | tf_op jit(solution)/shard_map/all_gather | solution.py:50
  61.6 149.3 %all-gather.17.cloned.1.call-start = ((), (), s32[]{:S(2)}) async-start(), calls=%async_computation.4 | async-start | bytes 4718592 | tf_op jit(solution)/shard_map/all_gather | solution.py:51
  63.6 330.1 %all-reduce.7.cloned.1.call-start = ((), (), s32[]{:S(2)}) async-start(), calls=%async_computation.6 | async-start | bytes 14680064 | tf_op jit(solution)/shard_map/psum | solution.py:210
  63.9 56.6 %copy-start.61 = (s32[256]{0:T(256)}, s32[256]{0:T(256)S(1)}, u32[]{:S(2)}) copy-start(s32[256]{0:T(256)S(1)} %iota_add_fusion.2) | copy-start | bytes 3076
  63.9 168.1 %copy-start.69 = (s32[512]{0:T(512)}, s32[512]{0:T(512)S(1)}, u32[]{:S(2)}) copy-start(s32[512]{0:T(512)S(1)} %fusion.125) | copy-start | bytes 6148
  68.7 163.3 %copy-start.63 = (s32[896]{0:T(1024)}, s32[896]{0:T(1024)S(1)}, u32[]{:S(2)}) copy-start(s32[896]{0:T(1024)S(1)} %broadcast_multiply_fusion.1) | copy-start | bytes 10756
  68.8 57.1 %copy-start.13 = (pred[128,1024]{1,0:T(8,128)(4,1)}, pred[128,1024]{1,0:T(8,128)(4,1)S(1)}, u32[]{:S(2)}) copy-start(pred[128,1024]{1,0:T(8,128)(4,1)S(1)} %iota_compare_fusion.3) | copy-start | bytes 393220
  69.2 147.9 %copy-start.6 = (pred[256,2048]{1,0:T(8,128)(4,1)}, pred[256,2048]{1,0:T(8,128)(4,1)S(1)}, u32[]{:S(2)}) copy-start(pred[256,2048]{1,0:T(8,128)(4,1)S(1)} %iota_compare_fusion.1) | copy-start | bytes 1572868
  185.7 42.5 %copy-start.48 = (f32[2,4,256]{2,1,0:T(4,128)}, f32[2,4,256]{2,1,0:T(4,128)S(1)}, u32[]{:S(2)}) copy-start(f32[2,4,256]{2,1,0:T(4,128)S(1)} %fusion) | copy-start | bytes 24580
  239.3 237.9 %all-gather.21.cloned.1.call-start = ((), (), s32[]{:S(2)}) async-start(), calls=%async_computation.7 | async-start | bytes 9437184 | tf_op jit(solution)/shard_map/all_gather | solution.py:214
  239.9 319.9 %all-gather.23.cloned.1.call-start = ((), (), s32[]{:S(2)}) async-start(), calls=%async_computation.8 | async-start | bytes 9437184 | tf_op jit(solution)/shard_map/all_gather | solution.py:215
  240.6 499.3 %all-reduce.9.cloned.1.call-start = ((), (), s32[]{:S(2)}) async-start(), calls=%async_computation.9 | async-start | bytes 14680064 | tf_op jit(solution)/shard_map/psum | solution.py:237
  240.7 319.1 %copy-start.59 = (s32[2048]{0:T(1024)}, s32[2048]{0:T(1024)S(1)}, u32[]{:S(2)}) copy-start(s32[2048]{0:T(1024)S(1)} %iota_add_fusion) | copy-start | bytes 24580
  240.7 319.1 %copy-start.65 = (s32[896]{0:T(1024)}, s32[896]{0:T(1024)S(1)}, u32[]{:S(2)}) copy-start(s32[896]{0:T(1024)S(1)} %broadcast_multiply_fusion) | copy-start | bytes 10756
  398.6 78.6 %copy-start.46 = (f32[2048]{0:T(1024)S(1)}, f32[2048]{0:T(1024)}, u32[]{:S(2)}) copy-start(f32[2048]{0:T(1024)} %param.18) | copy-start | bytes 24580
  586.1 216.8 %all-gather.25.cloned.1.call-start = ((), (), s32[]{:S(2)}) async-start(), calls=%async_computation.10 | async-start | bytes 3538944 | tf_op jit(solution)/shard_map/all_gather | solution.py:269
  588.3 239.0 %all-gather.29.cloned.1.call-start = ((), (), s32[]{:S(2)}) async-start(), calls=%async_computation.12 | async-start | bytes 4718592 | tf_op jit(solution)/shard_map/all_gather | solution.py:269
  589.8 355.7 %all-gather.27.cloned.1.call-start = ((), (), s32[]{:S(2)}) async-start(), calls=%async_computation.11 | async-start | bytes 3538944 | tf_op jit(solution)/shard_map/all_gather | solution.py:270
  758.4 203.5 %all-gather.31.cloned.1.call-start = ((), (), s32[]{:S(2)}) async-start(), calls=%async_computation.13 | async-start | bytes 4718592 | tf_op jit(solution)/shard_map/all_gather | solution.py:270
  760.6 303.3 %all-reduce.11.cloned.1.call-start = ((), (), s32[]{:S(2)}) async-start(), calls=%async_computation.14 | async-start | bytes 4194304 | tf_op jit(solution)/shard_map/psum | solution.py:325
  768.0 306.0 %reduce-scatter.5.cloned.1.call-start = ((), (), s32[]{:S(2)}) async-start(), calls=%async_computation.16 | async-start | bytes 9437184 | tf_op jit(solution)/shard_map/reduce_scatter | solution.py:244
  783.6 381.1 %reduce-scatter.3.cloned.1.call-start = ((), (), s32[]{:S(2)}) async-start(), calls=%async_computation.15 | async-start | bytes 9437184 | tf_op jit(solution)/shard_map/reduce_scatter | solution.py:241
  799.4 523.1 %all-reduce.13.cloned.1.call-start = ((), (), s32[]{:S(2)}) async-start(), calls=%async_computation.18 | async-start | bytes 14680064 | tf_op jit(solution)/shard_map/psum | solution.py:220
  827.0 25.4 %copy-start.20 = (bf16[512,4,128]{2,0,1:T(8,128)(2,1)S(1)}, bf16[512,4,128]{2,0,1:T(8,128)(2,1)}, u32[]{:S(2)}) copy-start(bf16[512,4,128]{2,0,1:T(8,128)(2,1)} %copy-done.19) | copy-start | bytes 1572868
  902.4 43.1 %copy-start.39 = (pred[1024,128]{1,0:T(8,128)(4,1)S(1)}, pred[1024,128]{1,0:T(8,128)(4,1)}, u32[]{:S(2)}) copy-start(pred[1024,128]{1,0:T(8,128)(4,1)} %iota_compare_fusion.2) | copy-start | bytes 393220
  1008.7 742.9 %all-gather.33.cloned.1.call-start = ((), (), s32[]{:S(2)}) async-start(), calls=%async_computation.17 | async-start | bytes 56623104 | tf_op jit(solution)/shard_map/all_gather | solution.py:322
  1027.4 34.4 %copy-start.38 = (f32[2048,8]{0,1:T(8,128)S(1)}, f32[2048,8]{0,1:T(8,128)}, u32[]{:S(2)}) copy-start(f32[2048,8]{0,1:T(8,128)} %param.19) | copy-start | bytes 196612
  1027.4 35.1 %copy-start.71 = (s32[5,2]{0,1:T(2,128)S(1)}, s32[5,2]{0,1:T(2,128)}, u32[]{:S(2)}) copy-start(s32[5,2]{0,1:T(2,128)} %param.22) | copy-start | bytes 124
  1751.6 29.4 %copy-start.1 = (bf16[512,2048]{1,0:T(8,128)(2,1)S(1)}, bf16[512,2048]{1,0:T(8,128)(2,1)}, u32[]{:S(2)}) copy-start(bf16[512,2048]{1,0:T(8,128)(2,1)} %param.14) | copy-start | bytes 6291460
  (58 other events, 357.6 us)
Sparse Core Ops, SparseCore 0:
  35.5 40.9 all-gather.12
  78.7 37.1 all-gather.14
  118.0 45.7 all-gather.18
  165.2 45.6 all-gather.16
  239.4 154.2 all-reduce.6
  395.1 82.0 all-gather.20
  478.8 80.9 all-gather.22
  586.2 153.5 all-reduce.8
  741.5 38.1 all-gather.24
  781.2 46.1 all-gather.28
  829.0 38.3 all-gather.26
  869.4 46.0 all-gather.30
  918.4 63.6 all-reduce.10
  984.2 89.6 reduce-scatter.4
  1076.7 87.9 reduce-scatter.2
  1168.6 153.8 all-reduce.12
  1324.0 427.5 all-gather.32
